TPU v7x, 32 devices: a whole 2x2x4 slice. The times are simulated.
32 devices in a mesh: dp: 8 (over z, core), own: 4 (over y, x).
Axes of the slice: x: 2, y: 2, z: 4, core: 2. Of those that a mesh axis runs over, the one named last changes fastest.
Arguments:
- tokens_in: bfloat16 [64, 256, 768], P(('dp', 'own')), may hold values from -6 to 6
- condition: float32 [64, 768], P(('dp', 'own')), may hold values from -6 to 6
- cotangent: bfloat16 [64, 256, 768], P(('dp', 'own')), may hold values from -6 to 6
- w_qkv: float32 [768, 2304], P('own', 'dp'), may hold values from -0.21875 to 0.21875
- w_proj: float32 [768, 768], P('own', 'dp'), may hold values from -0.625 to 0.625
- w_fc1: float32 [768, 3072], P('own', 'dp'), may hold values from -0.21875 to 0.21875
- w_fc2: float32 [3072, 768], P('dp', 'own'), may hold values from -0.109375 to 0.109375
- w_ada: float32 [768, 4608], P('own', 'dp'), may hold values from -0.21875 to 0.21875
- mom_qkv: float32 [768, 2304], P('own', 'dp'), may hold values from -384 to 384
- mom_proj: float32 [768, 768], P('own', 'dp'), may hold values from -384 to 384
- mom_fc1: float32 [768, 3072], P('own', 'dp'), may hold values from -384 to 384
- mom_fc2: float32 [3072, 768], P('dp', 'own'), may hold values from -384 to 384
- mom_ada: float32 [768, 4608], P('own', 'dp'), may hold values from -384 to 384
- biases: float32 [10752], P(('dp', 'own')), may hold values from -4 to 4
- bias_mom: float32 [10752], P(('dp', 'own')), may hold values from -224 to 224
Outputs:
- block_out: float32 [64, 256, 768], P(('dp', 'own'))
- grad_in: float32 [64, 256, 768], P(('dp', 'own'))
- grad_cond: float32 [64, 768], P(('dp', 'own'))
- grad_qkv: float32 [768, 2304], P('own', 'dp')
- grad_proj: float32 [768, 768], P('own', 'dp')
- grad_fc1: float32 [768, 3072], P('own', 'dp')
- grad_fc2: float32 [3072, 768], P('dp', 'own')
- grad_ada: float32 [768, 4608], P('own', 'dp')
- grad_bias: float32 [10752], P(('dp', 'own'))
- new_qkv: float32 [768, 2304], P('own', 'dp')
- new_proj: float32 [768, 768], P('own', 'dp')
- new_fc1: float32 [768, 3072], P('own', 'dp')
- new_fc2: float32 [3072, 768], P('dp', 'own')
- new_ada: float32 [768, 4608], P('own', 'dp')
- moment_qkv: float32 [768, 2304], P('own', 'dp')
- moment_proj: float32 [768, 768], P('own', 'dp')
- moment_fc1: float32 [768, 3072], P('own', 'dp')
- moment_fc2: float32 [3072, 768], P('dp', 'own')
- moment_ada: float32 [768, 4608], P('own', 'dp')
- new_bias: float32 [10752], P(('dp', 'own'))
- moment_bias: float32 [10752], P(('dp', 'own'))
- moment_norms: float32 [5], replicated
All inputs are finite; a program needn't handle non-finite values.
Results may differ from a plain program's by a relative error of at most 0.028.
Values may be sent and summed in bfloat16 or wider, within the bound.
No kernel may reach another device: no remote copies, remote signals or barrier semaphores. Data moves between devices by JAX's collectives and lax.ppermute only.
A program may use at most 192 MiB of HBM per device.

v0:
```python
import math
import jax
import jax.numpy as jnp
from jax import lax
from jax.sharding import PartitionSpec as P

HEADS = 12
NS_ITERS = 5
momentum_rate = 0.9
learn_rate = 0.15
bias_rate = 0.002
coef_first = 3.4445
coef_second = -4.775
coef_third = 2.0315
gelu_scale = math.sqrt(2.0 / math.pi)
norm_epsilon = 1e-06


def for_sending(array):
    return jax.tree.map(lambda a: a.astype(jnp.bfloat16) if a.dtype == jnp.float32 else a, array)


def batched(form, left, right):
    return jnp.einsum(form, left, right, preferred_element_type=jnp.float32)


def layer_stats(values):
    mean_value = jnp.mean(values, axis=-1, keepdims=True)
    centered = values - mean_value
    inv_std = lax.rsqrt(jnp.mean(centered * centered, axis=-1, keepdims=True) + norm_epsilon)
    return (centered * inv_std, inv_std)


def norm_back(grad_normed, normed, inv_std):
    first = jnp.mean(grad_normed, axis=-1, keepdims=True)
    second = jnp.mean(grad_normed * normed, axis=-1, keepdims=True)
    return inv_std * (grad_normed - first - normed * second)


def gelu_value(inner):
    return 0.5 * inner * (1.0 + jnp.tanh(gelu_scale * (inner + 0.044715 * inner * inner * inner)))


def gelu_slope(inner):
    tangent = jnp.tanh(gelu_scale * (inner + 0.044715 * inner * inner * inner))
    return 0.5 * (1.0 + tangent) + 0.5 * inner * (1.0 - tangent * tangent) * gelu_scale * (
        1.0 + 3.0 * 0.044715 * inner * inner
    )


def block_pass(tokens_in, condition, cotangent, w_qkv, w_proj, w_fc1, w_fc2, w_ada, bias_low):
    latents, length, features = tokens_in.shape
    hidden_units = w_fc1.shape[1]
    head_count = HEADS
    head_size = features // head_count
    score_scale = 1.0 / math.sqrt(head_size)
    row_count = latents * length
    bias_full = bias_low.astype(jnp.float32)
    b_query = bias_full[:features]
    b_value = bias_full[features : 2 * features]
    b_proj = bias_full[2 * features : 3 * features]
    b_fc1 = bias_full[3 * features : 3 * features + hidden_units]
    b_fc2 = bias_full[3 * features + hidden_units : 4 * features + hidden_units]
    b_ada = bias_full[4 * features + hidden_units :]
    cond_act = jax.nn.silu(condition).astype(jnp.bfloat16)
    modulation = jnp.dot(cond_act, w_ada, preferred_element_type=jnp.float32) + b_ada
    pieces = [
        modulation[:, index * features : (index + 1) * features][:, None, :] for index in range(6)
    ]
    shift_one, scale_one, gate_one, shift_two, scale_two, gate_two = pieces
    residual = tokens_in.astype(jnp.float32)
    normed_one, inv_one = layer_stats(residual)
    modulated_one = (normed_one * (1.0 + scale_one) + shift_one).astype(jnp.bfloat16)
    qkv_proj = jnp.dot(
        modulated_one.reshape(row_count, features), w_qkv, preferred_element_type=jnp.float32
    )
    qkv_proj = qkv_proj.reshape(latents, length, 3 * features)
    head_shape = (latents, length, head_count, head_size)
    query_heads = (qkv_proj[..., :features] + b_query).astype(jnp.bfloat16).reshape(head_shape)
    key_heads = qkv_proj[..., features : 2 * features].astype(jnp.bfloat16).reshape(head_shape)
    value_heads = (qkv_proj[..., 2 * features :] + b_value).astype(jnp.bfloat16).reshape(head_shape)
    scores = batched("bqhd,bkhd->bhqk", query_heads, key_heads) * score_scale
    row_max = jnp.max(scores, axis=-1, keepdims=True)
    log_total = row_max + jnp.log(jnp.sum(jnp.exp(scores - row_max), axis=-1, keepdims=True))
    attn_probs = jnp.exp(scores - log_total).astype(jnp.bfloat16)
    attn_out = (
        batched("bhqk,bkhd->bqhd", attn_probs, value_heads)
        .astype(jnp.bfloat16)
        .reshape(row_count, features)
    )
    branch_one = (jnp.dot(attn_out, w_proj, preferred_element_type=jnp.float32) + b_proj).reshape(
        latents, length, features
    )
    middle = residual + gate_one * branch_one
    normed_two, inv_two = layer_stats(middle)
    modulated_two = (
        (normed_two * (1.0 + scale_two) + shift_two)
        .astype(jnp.bfloat16)
        .reshape(row_count, features)
    )
    fc1_pre = jnp.dot(modulated_two, w_fc1, preferred_element_type=jnp.float32) + b_fc1
    fc1_act = gelu_value(fc1_pre).astype(jnp.bfloat16)
    branch_two = (jnp.dot(fc1_act, w_fc2, preferred_element_type=jnp.float32) + b_fc2).reshape(
        latents, length, features
    )
    block_out = middle + gate_two * branch_two
    cot_float = cotangent.astype(jnp.float32)
    d_gate_two = jnp.sum(cot_float * branch_two, axis=1)
    d_branch_two = cot_float * gate_two
    dbranch_low = d_branch_two.astype(jnp.bfloat16).reshape(row_count, features)
    g_fc2 = jnp.dot(fc1_act.T, dbranch_low, preferred_element_type=jnp.float32)
    gb_fc2 = jnp.sum(d_branch_two, axis=(0, 1))
    d_pre = jnp.dot(dbranch_low, w_fc2.T, preferred_element_type=jnp.float32) * gelu_slope(fc1_pre)
    dpre_low = d_pre.astype(jnp.bfloat16)
    g_fc1 = jnp.dot(modulated_two.T, dpre_low, preferred_element_type=jnp.float32)
    gb_fc1 = jnp.sum(d_pre, axis=0)
    d_mod_two = jnp.dot(dpre_low, w_fc1.T, preferred_element_type=jnp.float32).reshape(
        latents, length, features
    )
    d_shift_two = jnp.sum(d_mod_two, axis=1)
    d_scale_two = jnp.sum(d_mod_two * normed_two, axis=1)
    d_middle = cot_float + norm_back(d_mod_two * (1.0 + scale_two), normed_two, inv_two)
    d_gate_one = jnp.sum(d_middle * branch_one, axis=1)
    d_branch_one = d_middle * gate_one
    dbranch_one_low = d_branch_one.astype(jnp.bfloat16).reshape(row_count, features)
    g_proj = jnp.dot(attn_out.T, dbranch_one_low, preferred_element_type=jnp.float32)
    gb_proj = jnp.sum(d_branch_one, axis=(0, 1))
    d_attn = (
        jnp.dot(dbranch_one_low, w_proj.T, preferred_element_type=jnp.float32)
        .astype(jnp.bfloat16)
        .reshape(head_shape)
    )
    scores_again = batched("bqhd,bkhd->bhqk", query_heads, key_heads) * score_scale
    probs_again = jnp.exp(scores_again - log_total)
    d_probs = batched("bqhd,bkhd->bhqk", d_attn, value_heads)
    delta = jnp.sum(probs_again * d_probs, axis=-1, keepdims=True)
    d_scores = (probs_again * (d_probs - delta) * score_scale).astype(jnp.bfloat16)
    d_query = batched("bhqk,bkhd->bqhd", d_scores, key_heads)
    d_key = batched("bhqk,bqhd->bkhd", d_scores, query_heads)
    d_value = batched("bhqk,bqhd->bkhd", probs_again.astype(jnp.bfloat16), d_attn)
    flat_shape = (latents, length, features)
    d_qkv = jnp.concatenate(
        [d_query.reshape(flat_shape), d_key.reshape(flat_shape), d_value.reshape(flat_shape)],
        axis=-1,
    )
    dqkv_low = d_qkv.astype(jnp.bfloat16).reshape(row_count, 3 * features)
    g_qkv = jnp.dot(
        modulated_one.reshape(row_count, features).T, dqkv_low, preferred_element_type=jnp.float32
    )
    gb_query = jnp.sum(d_query, axis=(0, 1)).reshape(features)
    gb_value = jnp.sum(d_value, axis=(0, 1)).reshape(features)
    d_mod_one = jnp.dot(dqkv_low, w_qkv.T, preferred_element_type=jnp.float32).reshape(flat_shape)
    d_shift_one = jnp.sum(d_mod_one, axis=1)
    d_scale_one = jnp.sum(d_mod_one * normed_one, axis=1)
    grad_in = d_middle + norm_back(d_mod_one * (1.0 + scale_one), normed_one, inv_one)
    d_modulation = jnp.concatenate(
        [d_shift_one, d_scale_one, d_gate_one, d_shift_two, d_scale_two, d_gate_two], axis=-1
    )
    dmod_low = d_modulation.astype(jnp.bfloat16)
    g_ada = jnp.dot(cond_act.T, dmod_low, preferred_element_type=jnp.float32)
    gb_ada = jnp.sum(d_modulation, axis=0)
    sigmoid_c = jax.nn.sigmoid(condition)
    grad_cond = jnp.dot(dmod_low, w_ada.T, preferred_element_type=jnp.float32) * (
        sigmoid_c * (1.0 + condition * (1.0 - sigmoid_c))
    )
    grad_bias = jnp.concatenate([gb_query, gb_value, gb_proj, gb_fc1, gb_fc2, gb_ada])
    return (
        block_out,
        grad_in,
        grad_cond,
        (g_qkv, g_proj, g_fc1, g_fc2, g_ada),
        grad_bias,
        cond_act,
        dmod_low,
    )


def per_device(
    tokens_in,
    condition,
    cotangent,
    w_qkv,
    w_proj,
    w_fc1,
    w_fc2,
    w_ada,
    mom_qkv,
    mom_proj,
    mom_fc1,
    mom_fc2,
    mom_ada,
    biases,
    bias_mom,
):
    own_part = (
        lax.all_gather(w_qkv.astype(jnp.bfloat16), "own", axis=0, tiled=True),
        lax.all_gather(w_proj.astype(jnp.bfloat16), "own", axis=0, tiled=True),
        lax.all_gather(w_fc1.astype(jnp.bfloat16), "own", axis=0, tiled=True),
        lax.all_gather(w_fc2.astype(jnp.bfloat16), "own", axis=1, tiled=True),
        lax.all_gather(w_ada.astype(jnp.bfloat16), "own", axis=0, tiled=True),
        lax.all_gather(biases.astype(jnp.bfloat16), "own", axis=0, tiled=True),
    )
    full = (
        lax.all_gather(own_part[0], "dp", axis=1, tiled=True),
        lax.all_gather(own_part[1], "dp", axis=1, tiled=True),
        lax.all_gather(own_part[2], "dp", axis=1, tiled=True),
        lax.all_gather(own_part[3], "dp", axis=0, tiled=True),
        lax.all_gather(own_part[4], "dp", axis=1, tiled=True),
        lax.all_gather(own_part[5], "dp", axis=0, tiled=True),
    )
    block_out, grad_in, grad_cond, partials, bias_terms, cond_act, dmod_low = block_pass(
        tokens_in, condition, cotangent, full[0], full[1], full[2], full[3], full[4], full[5]
    )
    summed = (
        lax.psum_scatter(partials[0], "dp", scatter_dimension=1, tiled=True),
        lax.psum_scatter(partials[1], "dp", scatter_dimension=1, tiled=True),
        lax.psum_scatter(partials[2], "dp", scatter_dimension=1, tiled=True),
        lax.psum_scatter(partials[3], "dp", scatter_dimension=0, tiled=True),
        lax.psum_scatter(partials[4], "dp", scatter_dimension=1, tiled=True),
        lax.psum_scatter(bias_terms, "dp", scatter_dimension=0, tiled=True),
    )
    owned = (
        lax.psum_scatter(summed[0], "own", scatter_dimension=0, tiled=True),
        lax.psum_scatter(summed[1], "own", scatter_dimension=0, tiled=True),
        lax.psum_scatter(summed[2], "own", scatter_dimension=0, tiled=True),
        lax.psum_scatter(summed[3], "own", scatter_dimension=1, tiled=True),
        lax.psum_scatter(summed[4], "own", scatter_dimension=0, tiled=True),
        lax.psum_scatter(summed[5], "own", scatter_dimension=0, tiled=True),
    )
    tiles = (owned[0], owned[1], owned[2], owned[3], owned[4])
    bias_tile = owned[5]
    weights = (w_qkv, w_proj, w_fc1, w_fc2, w_ada)
    moments = (mom_qkv, mom_proj, mom_fc1, mom_fc2, mom_ada)
    fresh = [momentum_rate * moments[index] + tiles[index] for index in range(5)]
    oriented = [fresh[0], fresh[1], fresh[2], fresh[3].T, fresh[4]]
    squares = lax.psum(
        (
            jnp.sum(oriented[0] * oriented[0]),
            jnp.sum(oriented[1] * oriented[1]),
            jnp.sum(oriented[2] * oriented[2]),
            jnp.sum(oriented[3] * oriented[3]),
            jnp.sum(oriented[4] * oriented[4]),
        ),
        ("dp", "own"),
    )
    magnitudes = [jnp.sqrt(squares[index]) for index in range(5)]
    moment_norms = jnp.stack(magnitudes)
    iterate = [oriented[index] / (magnitudes[index] + 1e-07) for index in range(5)]
    highest = lax.Precision.HIGHEST
    for ns_step in range(NS_ITERS):
        columns = (
            lax.all_gather(for_sending(iterate[0]), "own", axis=0, tiled=True),
            lax.all_gather(for_sending(iterate[1]), "own", axis=0, tiled=True),
            lax.all_gather(for_sending(iterate[2]), "own", axis=0, tiled=True),
            lax.all_gather(for_sending(iterate[3]), "own", axis=0, tiled=True),
            lax.all_gather(for_sending(iterate[4]), "own", axis=0, tiled=True),
        )
        products = [
            jnp.dot(iterate[index], columns[index].T, precision=highest) for index in range(5)
        ]
        grams = (
            lax.psum(products[0].astype(jnp.bfloat16), "dp").astype(jnp.float32),
            lax.psum(products[1].astype(jnp.bfloat16), "dp").astype(jnp.float32),
            lax.psum(products[2].astype(jnp.bfloat16), "dp").astype(jnp.float32),
            lax.psum(products[3].astype(jnp.bfloat16), "dp").astype(jnp.float32),
            lax.psum(products[4].astype(jnp.bfloat16), "dp").astype(jnp.float32),
        )
        gram_full = (
            lax.all_gather(grams[0].astype(jnp.bfloat16), "own", axis=0, tiled=True).astype(
                jnp.float32
            ),
            lax.all_gather(grams[1].astype(jnp.bfloat16), "own", axis=0, tiled=True).astype(
                jnp.float32
            ),
            lax.all_gather(grams[2].astype(jnp.bfloat16), "own", axis=0, tiled=True).astype(
                jnp.float32
            ),
            lax.all_gather(grams[3].astype(jnp.bfloat16), "own", axis=0, tiled=True).astype(
                jnp.float32
            ),
            lax.all_gather(grams[4].astype(jnp.bfloat16), "own", axis=0, tiled=True).astype(
                jnp.float32
            ),
        )
        next_iterate = []
        for index in range(5):
            square = jnp.dot(grams[index], gram_full[index], precision=highest)
            mixer = coef_second * grams[index] + coef_third * square
            updated = coef_first * iterate[index] + jnp.dot(
                mixer, columns[index], precision=highest
            )
            next_iterate.append(updated)
        iterate = next_iterate
    ortho = [iterate[0], iterate[1], iterate[2], iterate[3].T, iterate[4]]
    updated_weights = []
    for index in range(5):
        whole_shape = full[index].shape
        factor = 0.2 * math.sqrt(max(whole_shape[0], whole_shape[1]))
        updated_weights.append(weights[index] - learn_rate * factor * ortho[index])
    moment_bias = momentum_rate * bias_mom + bias_tile
    new_bias = biases - bias_rate * moment_bias
    return (
        block_out,
        grad_in,
        grad_cond,
        tiles[0],
        tiles[1],
        tiles[2],
        tiles[3],
        tiles[4],
        bias_tile,
        updated_weights[0],
        updated_weights[1],
        updated_weights[2],
        updated_weights[3],
        updated_weights[4],
        fresh[0],
        fresh[1],
        fresh[2],
        fresh[3],
        fresh[4],
        new_bias,
        moment_bias,
        moment_norms,
    )


def solution(mesh):
    placed = (
        P(("dp", "own"), None, None),
        P(("dp", "own"), None),
        P(("dp", "own"), None, None),
        P("own", "dp"),
        P("own", "dp"),
        P("own", "dp"),
        P("dp", "own"),
        P("own", "dp"),
        P("own", "dp"),
        P("own", "dp"),
        P("own", "dp"),
        P("dp", "own"),
        P("own", "dp"),
        P(("dp", "own")),
        P(("dp", "own")),
    )
    return jax.shard_map(
        per_device,
        mesh=mesh,
        in_specs=placed,
        out_specs=(
            P(("dp", "own"), None, None),
            P(("dp", "own"), None, None),
            P(("dp", "own"), None),
            P("own", "dp"),
            P("own", "dp"),
            P("own", "dp"),
            P("dp", "own"),
            P("own", "dp"),
            P(("dp", "own")),
            P("own", "dp"),
            P("own", "dp"),
            P("own", "dp"),
            P("dp", "own"),
            P("own", "dp"),
            P("own", "dp"),
            P("own", "dp"),
            P("own", "dp"),
            P("dp", "own"),
            P("own", "dp"),
            P(("dp", "own")),
            P(("dp", "own")),
            P(),
        ),
        check_vma=False,
    )
```

profile of v0, /device:TPU:0, one launch (start us, length us, event | category | flops | bytes accessed | tf_op | source)
XLA Modules:
  0.0 2185.7 jit_solution(3009070349646886199)
XLA Ops:
  78.5 27.1 %all-reduce.1 = bf16[10752]{0:T(1024)(128)(2,1)S(1)} all-reduce(bf16[10752]{0:T(1024)(128)(2,1)S(1)} %dynamic-update-slice.1), channel_id=1, replica_groups=mesh['dp'=8,'own'=4] {'dp'}, use_global_device_ids=true, to_apply=%add.1 | all-reduce | flops 10752 | bytes 43008
  111.3 27.0 %all-gather.33.cloned.1.call-done = bf16[768,2304]{0,1:T(8,128)(2,1)} async-done(((bf16[768,288]{0,1:T(8,128)(2,1)}), bf16[768,2304]{0,1:T(8,128)(2,1)}) %all-gather.33.cloned.1.call-update) | async-done | bytes 3538960 | tf_op jit(solution)/shard_map/all_gather | solution.py:204
  167.1 47.7 %all-gather.37.cloned.1.call-done = bf16[768,3072]{1,0:T(8,128)(2,1)} async-done(((bf16[768,384]{1,0:T(8,128)(2,1)}), bf16[768,3072]{1,0:T(8,128)(2,1)}) %all-gather.37.cloned.1.call-update) | async-done | bytes 4718608 | tf_op jit(solution)/shard_map/all_gather | solution.py:206
  221.7 44.7 %all-gather.39.cloned.1.call-done = bf16[3072,768]{0,1:T(8,128)(2,1)} async-done(((bf16[384,768]{0,1:T(8,128)(2,1)}), bf16[3072,768]{0,1:T(8,128)(2,1)}) %all-gather.39.cloned.1.call-update) | async-done | bytes 4718608 | tf_op jit(solution)/shard_map/all_gather | solution.py:207
  376.8 39.7 %reduce-scatter.17.cloned.1.call-done = f32[768,288]{0,1:T(8,128)} async-done(((f32[768,2304]{0,1:T(8,128)}), f32[768,288]{0,1:T(8,128)}) %reduce-scatter.17.cloned.1.call-update) | async-done | bytes 884752 | tf_op jit(solution)/shard_map/reduce_scatter | solution.py:215
  419.2 97.6 %reduce-scatter.21.cloned.1.call-done = f32[768,384]{1,0:T(8,128)} async-done(((f32[768,3072]{1,0:T(8,128)}), f32[768,384]{1,0:T(8,128)}) %reduce-scatter.21.cloned.1.call-update) | async-done | bytes 1179664 | tf_op jit(solution)/shard_map/reduce_scatter | solution.py:217
  516.9 100.2 %reduce-scatter.25.cloned.1.call-done = f32[384,768]{0,1:T(8,128)} async-done(((f32[3072,768]{0,1:T(8,128)}), f32[384,768]{0,1:T(8,128)}) %reduce-scatter.25.cloned.1.call-update) | async-done | bytes 1179664 | tf_op jit(solution)/shard_map/reduce_scatter | solution.py:218
  617.1 144.6 %reduce-scatter.29.cloned.1.call-done = f32[768,576]{0,1:T(8,128)} async-done(((f32[768,4608]{0,1:T(8,128)}), f32[768,576]{0,1:T(8,128)}) %reduce-scatter.29.cloned.1.call-update) | async-done | bytes 1769488 | tf_op jit(solution)/shard_map/reduce_scatter | solution.py:219
  764.6 24.2 %reduce-scatter.33.cloned.1.call-done = f32[192,96]{1,0:T(8,128)} async-done(((f32[768,96]{1,0:T(8,128)}), f32[192,96]{1,0:T(8,128)}) %reduce-scatter.33.cloned.1.call-update) | async-done | bytes 73744
  790.3 30.6 %reduce-scatter.31.cloned.1.call-done = f32[192,288]{1,0:T(8,128)} async-done(((f32[768,288]{1,0:T(8,128)}), f32[192,288]{1,0:T(8,128)}) %reduce-scatter.31.cloned.1.call-update) | async-done | bytes 221200
  822.6 30.6 %reduce-scatter.23.cloned.1.call-done = f32[192,384]{1,0:T(8,128)} async-done(((f32[768,384]{1,0:T(8,128)}), f32[192,384]{1,0:T(8,128)}) %reduce-scatter.23.cloned.1.call-update) | async-done | bytes 294928 | tf_op jit(solution)/shard_map/reduce_scatter | solution.py:225
  854.8 30.5 %reduce-scatter.27.cloned.1.call-done = f32[384,192]{0,1:T(8,128)} async-done(((f32[384,768]{0,1:T(8,128)}), f32[384,192]{0,1:T(8,128)}) %reduce-scatter.27.cloned.1.call-update) | async-done | bytes 294928 | tf_op jit(solution)/shard_map/reduce_scatter | solution.py:226
  886.9 36.0 %reduce-scatter.35.cloned.1.call-done = f32[192,576]{1,0:T(8,128)} async-done(((f32[768,576]{1,0:T(8,128)}), f32[192,576]{1,0:T(8,128)}) %reduce-scatter.35.cloned.1.call-update) | async-done | bytes 442384
  924.7 39.7 %all-reduce.4 = (f32[]{:T(128)}, f32[]{:T(128)}, f32[]{:T(128)}, f32[]{:T(128)}, f32[]{:T(128)}) all-reduce(f32[]{:T(128)} %get-tuple-element.188, f32[]{:T(128)} %get-tuple-element.186, f32[]{:T(128)} %get-tuple-element.184, f32[]{:T(128)} %get-tuple-element.182, f32[]{:T(128)} %get-tuple-element.180), channel_id=1, replica_groups=mesh['dp'=8,'own'=4] {'dp','own'}, use_global_device_ids=true, to_apply=%region_36.37 | all-reduce | flops 5 | bytes 40 | tf_op jit(solution)/shard_map/psum | solution.py:236
  1028.5 60.7 %all-reduce.24.cloned.1.call-done = (bf16[192,768]{1,0:T(8,128)(2,1)}, bf16[192,768]{1,0:T(8,128)(2,1)}, bf16[192,768]{1,0:T(8,128)(2,1)}, bf16[192,768]{1,0:T(8,128)(2,1)}, bf16[192,768]{1,0:T(8,128)(2,1)}) async-done(((bf16[192,768]{1,0:T(8,128)(2,1)}, bf16[192,768]{1,0:T(8,128)(2,1)}, bf16[192,768]{1,0:T(8,128)(2,1)}, bf16[192,768]{1,0:T(8,128)(2,1)}, bf16[192,768]{1,0:T(8,128)(2,1)}), ...) | async-done | bytes 1474576 | tf_op jit(solution)/shard_map/psum | solution.py:262
  1092.0 26.2 %all-gather.51.cloned.1.call-done = bf16[768,768]{1,0:T(8,128)(2,1)} async-done(((bf16[192,768]{1,0:T(8,128)(2,1)}), bf16[768,768]{1,0:T(8,128)(2,1)}) %all-gather.51.cloned.1.call-update) | async-done | bytes 1179664 | tf_op jit(solution)/shard_map/all_gather | solution.py:272
  1130.8 16.8 all-gather.71.cloned.1.call-done
  1212.8 15.9 all_gather.240
  1262.4 61.8 %all-reduce.22.cloned.1.call-done = (bf16[192,768]{1,0:T(8,128)(2,1)}, bf16[192,768]{1,0:T(8,128)(2,1)}, bf16[192,768]{1,0:T(8,128)(2,1)}, bf16[192,768]{1,0:T(8,128)(2,1)}, bf16[192,768]{1,0:T(8,128)(2,1)}) async-done(((bf16[192,768]{1,0:T(8,128)(2,1)}, bf16[192,768]{1,0:T(8,128)(2,1)}, bf16[192,768]{1,0:T(8,128)(2,1)}, bf16[192,768]{1,0:T(8,128)(2,1)}, bf16[192,768]{1,0:T(8,128)(2,1)}), ...) | async-done | bytes 1474576 | tf_op jit(solution)/shard_map/psum | solution.py:262
  1326.7 26.5 %all-gather.53.cloned.1.call-done = bf16[768,768]{1,0:T(8,128)(2,1)} async-done(((bf16[192,768]{1,0:T(8,128)(2,1)}), bf16[768,768]{1,0:T(8,128)(2,1)}) %all-gather.53.cloned.1.call-update) | async-done | bytes 1179664 | tf_op jit(solution)/shard_map/all_gather | solution.py:272
  1365.9 16.8 all-gather.73.cloned.1.call-done
  1496.4 61.6 %all-reduce.20.cloned.1.call-done = (bf16[192,768]{1,0:T(8,128)(2,1)}, bf16[192,768]{1,0:T(8,128)(2,1)}, bf16[192,768]{1,0:T(8,128)(2,1)}, bf16[192,768]{1,0:T(8,128)(2,1)}, bf16[192,768]{1,0:T(8,128)(2,1)}) async-done(((bf16[192,768]{1,0:T(8,128)(2,1)}, bf16[192,768]{1,0:T(8,128)(2,1)}, bf16[192,768]{1,0:T(8,128)(2,1)}, bf16[192,768]{1,0:T(8,128)(2,1)}, bf16[192,768]{1,0:T(8,128)(2,1)}), ...) | async-done | bytes 1474576 | tf_op jit(solution)/shard_map/psum | solution.py:262
  1560.7 26.3 %all-gather.55.cloned.1.call-done = bf16[768,768]{1,0:T(8,128)(2,1)} async-done(((bf16[192,768]{1,0:T(8,128)(2,1)}), bf16[768,768]{1,0:T(8,128)(2,1)}) %all-gather.55.cloned.1.call-update) | async-done | bytes 1179664 | tf_op jit(solution)/shard_map/all_gather | solution.py:272
  1599.9 16.7 all-gather.75.cloned.1.call-done
  1682.0 15.9 all_gather.244
  1731.5 61.7 %all-reduce.18.cloned.1.call-done = (bf16[192,768]{1,0:T(8,128)(2,1)}, bf16[192,768]{1,0:T(8,128)(2,1)}, bf16[192,768]{1,0:T(8,128)(2,1)}, bf16[192,768]{1,0:T(8,128)(2,1)}, bf16[192,768]{1,0:T(8,128)(2,1)}) async-done(((bf16[192,768]{1,0:T(8,128)(2,1)}, bf16[192,768]{1,0:T(8,128)(2,1)}, bf16[192,768]{1,0:T(8,128)(2,1)}, bf16[192,768]{1,0:T(8,128)(2,1)}, bf16[192,768]{1,0:T(8,128)(2,1)}), ...) | async-done | bytes 1474576 | tf_op jit(solution)/shard_map/psum | solution.py:262
  1795.8 26.5 %all-gather.57.cloned.1.call-done = bf16[768,768]{1,0:T(8,128)(2,1)} async-done(((bf16[192,768]{1,0:T(8,128)(2,1)}), bf16[768,768]{1,0:T(8,128)(2,1)}) %all-gather.57.cloned.1.call-update) | async-done | bytes 1179664 | tf_op jit(solution)/shard_map/all_gather | solution.py:272
  1834.5 17.1 all-gather.77.cloned.1.call-done
  1967.3 61.7 %all-reduce.16.cloned.1.call-done = (bf16[192,768]{1,0:T(8,128)(2,1)}, bf16[192,768]{1,0:T(8,128)(2,1)}, bf16[192,768]{1,0:T(8,128)(2,1)}, bf16[192,768]{1,0:T(8,128)(2,1)}, bf16[192,768]{1,0:T(8,128)(2,1)}) async-done(((bf16[192,768]{1,0:T(8,128)(2,1)}, bf16[192,768]{1,0:T(8,128)(2,1)}, bf16[192,768]{1,0:T(8,128)(2,1)}, bf16[192,768]{1,0:T(8,128)(2,1)}, bf16[192,768]{1,0:T(8,128)(2,1)}), ...) | async-done | bytes 1474576 | tf_op jit(solution)/shard_map/psum | solution.py:262
  2045.8 27.6 %all-reduce.2 = f32[10752]{0:T(1024)} all-reduce(f32[10752]{0:T(1024)} %constant_dynamic-update-slice_fusion.10), channel_id=12, replica_groups=mesh['dp'=8,'own'=4] {'dp'}, use_global_device_ids=true, to_apply=%region_33.34.clone | all-reduce | flops 10752 | bytes 86016
  2120.1 26.2 %all-gather.89.cloned.1.call-done = bf16[768,768]{1,0:T(8,128)(2,1)} async-done(((bf16[192,768]{1,0:T(8,128)(2,1)}), bf16[768,768]{1,0:T(8,128)(2,1)}) %all-gather.89.cloned.1.call-update) | async-done | bytes 1179664 | tf_op jit(solution)/shard_map/all_gather | solution.py:281
  2149.8 25.8 %all-gather.79.cloned.1.call-done = bf16[768,768]{1,0:T(8,128)(2,1)} async-done(((bf16[192,768]{1,0:T(8,128)(2,1)}), bf16[768,768]{1,0:T(8,128)(2,1)}) %all-gather.79.cloned.1.call-update) | async-done | bytes 1179664 | tf_op jit(solution)/shard_map/all_gather | solution.py:278
  (579 shorter events, 851.1 us)
Async XLA Ops:
  7.2 99.2 %all-gather.31.cloned.1.call-start = ((), (), s32[]{:S(2)}) async-start(), calls=%async_computation.10 | async-start | bytes 7962624 | tf_op jit(solution)/shard_map/all_gather | solution.py:208
  24.0 114.3 %all-gather.33.cloned.1.call-start = ((), (), s32[]{:S(2)}) async-start(), calls=%async_computation.11 | async-start | bytes 3981312 | tf_op jit(solution)/shard_map/all_gather | solution.py:204
  36.4 125.9 %all-gather.35.cloned.1.call-start = ((), (), s32[]{:S(2)}) async-start(), calls=%async_computation.12 | async-start | bytes 1327104 | tf_op jit(solution)/shard_map/all_gather | solution.py:205
  44.6 170.2 %all-gather.37.cloned.1.call-start = ((), (), s32[]{:S(2)}) async-start(), calls=%async_computation.13 | async-start | bytes 5308416 | tf_op jit(solution)/shard_map/all_gather | solution.py:206
  56.4 210.0 %all-gather.39.cloned.1.call-start = ((), (), s32[]{:S(2)}) async-start(), calls=%async_computation.14 | async-start | bytes 5308416 | tf_op jit(solution)/shard_map/all_gather | solution.py:207
  67.1 307.8 %reduce-scatter.19.cloned.1.call-start = ((), (), s32[]{:S(2)}) async-start(), calls=%async_computation.16 | async-start | bytes 2654208 | tf_op jit(solution)/shard_map/reduce_scatter | solution.py:216
  294.5 122.1 %reduce-scatter.17.cloned.1.call-start = ((), (), s32[]{:S(2)}) async-start(), calls=%async_computation.15 | async-start | bytes 7962624 | tf_op jit(solution)/shard_map/reduce_scatter | solution.py:215
  340.5 176.3 %reduce-scatter.21.cloned.1.call-start = ((), (), s32[]{:S(2)}) async-start(), calls=%async_computation.17 | async-start | bytes 10616832 | tf_op jit(solution)/shard_map/reduce_scatter | solution.py:217
  348.7 268.4 %reduce-scatter.25.cloned.1.call-start = ((), (), s32[]{:S(2)}) async-start(), calls=%async_computation.19 | async-start | bytes 10616832 | tf_op jit(solution)/shard_map/reduce_scatter | solution.py:218
  359.2 402.4 %reduce-scatter.29.cloned.1.call-start = ((), (), s32[]{:S(2)}) async-start(), calls=%async_computation.21 | async-start | bytes 15925248 | tf_op jit(solution)/shard_map/reduce_scatter | solution.py:219
  374.8 414.0 %reduce-scatter.33.cloned.1.call-start = ((), (), s32[]{:S(2)}) async-start(), calls=%async_computation.48 | async-start | bytes 491520
  376.8 444.2 %reduce-scatter.31.cloned.1.call-start = ((), (), s32[]{:S(2)}) async-start(), calls=%async_computation.47 | async-start | bytes 1474560
  419.1 434.0 %reduce-scatter.23.cloned.1.call-start = ((), (), s32[]{:S(2)}) async-start(), calls=%async_computation.18 | async-start | bytes 1474560 | tf_op jit(solution)/shard_map/reduce_scatter | solution.py:225
  516.8 368.5 %reduce-scatter.27.cloned.1.call-start = ((), (), s32[]{:S(2)}) async-start(), calls=%async_computation.20 | async-start | bytes 1474560 | tf_op jit(solution)/shard_map/reduce_scatter | solution.py:226
  617.1 305.9 %reduce-scatter.35.cloned.1.call-start = ((), (), s32[]{:S(2)}) async-start(), calls=%async_computation.49 | async-start | bytes 2457600
  764.5 324.7 %all-reduce.24.cloned.1.call-start = ((), (), s32[]{:S(2)}) async-start(), calls=%async_computation.54 | async-start | bytes 2949120 | tf_op jit(solution)/shard_map/psum | solution.py:262
  1090.6 118.7 %all-gather.81.cloned.1.call-start = ((), (), s32[]{:S(2)}) async-start(), calls=%async_computation.42 | async-start | bytes 1474560 | tf_op jit(solution)/shard_map/all_gather | solution.py:281
  1091.2 150.6 %all-gather.41.cloned.1.call-start = ((), (), s32[]{:S(2)}) async-start(), calls=%async_computation.22 | async-start | bytes 1474560 | tf_op jit(solution)/shard_map/all_gather | solution.py:269
  1091.9 232.2 %all-reduce.22.cloned.1.call-start = ((), (), s32[]{:S(2)}) async-start(), calls=%async_computation.53 | async-start | bytes 2949120 | tf_op jit(solution)/shard_map/psum | solution.py:262
  1262.3 90.9 %all-gather.53.cloned.1.call-start = ((), (), s32[]{:S(2)}) async-start(), calls=%async_computation.28 | async-start | bytes 1474560 | tf_op jit(solution)/shard_map/all_gather | solution.py:272
  1325.5 118.2 %all-gather.83.cloned.1.call-start = ((), (), s32[]{:S(2)}) async-start(), calls=%async_computation.43 | async-start | bytes 1474560 | tf_op jit(solution)/shard_map/all_gather | solution.py:281
  1326.1 150.0 %all-gather.43.cloned.1.call-start = ((), (), s32[]{:S(2)}) async-start(), calls=%async_computation.23 | async-start | bytes 1474560 | tf_op jit(solution)/shard_map/all_gather | solution.py:269
  1326.7 231.3 %all-reduce.20.cloned.1.call-start = ((), (), s32[]{:S(2)}) async-start(), calls=%async_computation.52 | async-start | bytes 2949120 | tf_op jit(solution)/shard_map/psum | solution.py:262
  1559.3 119.2 %all-gather.85.cloned.1.call-start = ((), (), s32[]{:S(2)}) async-start(), calls=%async_computation.44 | async-start | bytes 1474560 | tf_op jit(solution)/shard_map/all_gather | solution.py:281
  1560.1 150.8 %all-gather.45.cloned.1.call-start = ((), (), s32[]{:S(2)}) async-start(), calls=%async_computation.24 | async-start | bytes 1474560 | tf_op jit(solution)/shard_map/all_gather | solution.py:269
  1560.7 232.6 %all-reduce.18.cloned.1.call-start = ((), (), s32[]{:S(2)}) async-start(), calls=%async_computation.51 | async-start | bytes 2949120 | tf_op jit(solution)/shard_map/psum | solution.py:262
  1794.4 118.9 %all-gather.87.cloned.1.call-start = ((), (), s32[]{:S(2)}) async-start(), calls=%async_computation.45 | async-start | bytes 1474560 | tf_op jit(solution)/shard_map/all_gather | solution.py:281
  1795.2 150.6 %all-gather.47.cloned.1.call-start = ((), (), s32[]{:S(2)}) async-start(), calls=%async_computation.25 | async-start | bytes 1474560 | tf_op jit(solution)/shard_map/all_gather | solution.py:269
  1795.7 233.3 %all-reduce.16.cloned.1.call-start = ((), (), s32[]{:S(2)}) async-start(), calls=%async_computation.50 | async-start | bytes 2949120 | tf_op jit(solution)/shard_map/psum | solution.py:262
  1967.3 129.2 %all-gather.59.cloned.1.call-start = ((), (), s32[]{:S(2)}) async-start(), calls=%async_computation.31 | async-start | bytes 1474560 | tf_op jit(solution)/shard_map/all_gather | solution.py:272
  2030.4 115.9 %all-gather.89.cloned.1.call-start = ((), (), s32[]{:S(2)}) async-start(), calls=%async_computation.46 | async-start | bytes 1474560 | tf_op jit(solution)/shard_map/all_gather | solution.py:281
  2043.1 132.5 %all-gather.79.cloned.1.call-start = ((), (), s32[]{:S(2)}) async-start(), calls=%async_computation.41 | async-start | bytes 1474560 | tf_op jit(solution)/shard_map/all_gather | solution.py:278
  (143 other events, 5405.2 us)
Sparse Core Ops, SparseCore 0:
  24.2 71.8 all-gather.30
  98.2 40.0 all-gather.32
  163.7 51.0 all-gather.36
  216.3 50.0 all-gather.38
  294.6 35.5 reduce-scatter.18
  340.7 75.8 reduce-scatter.16
  418.9 97.8 reduce-scatter.20
  519.1 97.8 reduce-scatter.24
  619.2 142.4 reduce-scatter.28
  792.1 28.7 reduce-scatter.30
  824.4 28.7 reduce-scatter.22
  856.5 28.7 reduce-scatter.26
  888.8 34.1 reduce-scatter.34
  1028.6 60.6 all-reduce.23
  1119.8 27.7 all-gather.70
  1149.4 29.0 all-gather.60
  1180.2 29.1 all-gather.80
  1211.2 30.5 all-gather.40
  1262.5 61.6 all-reduce.21
  1384.5 28.2 all-gather.62
  1414.5 29.1 all-gather.82
  1445.4 30.5 all-gather.42
  1496.5 61.4 all-reduce.19
  1588.7 27.7 all-gather.74
  1618.4 29.1 all-gather.64
  1649.4 29.0 all-gather.84
  1680.2 30.6 all-gather.44
  1731.5 61.6 all-reduce.17
  1853.3 29.1 all-gather.66
  1884.3 28.9 all-gather.86
  1915.0 30.6 all-gather.46
  1967.4 61.6 all-reduce.15
  (13 shorter events, 345.5 us)
where the time goes:
time: 2190 us
  waiting for transfers between devices  1390 us (63%)
  blocking collectives  472 us (22%)
  matrix products  231 us (11%)
  local copies, waits for them, and re-layouts  43.6 us (2%)
  other arithmetic  26.6 us (1%)
  between operations  22.4 us (1%)
    psum x5, waiting for transfers between devices, per_device(): lax.psum(products[0].astype(jnp.bfloat16), 'dp').astype(jnp.float32)  308 us
    reduce_scatter x1, waiting for transfers between devices, per_device(): lax.psum_scatter(partials[4], 'dp', scatter_dimension=1, tiled=True)  145 us
    all_gather x5, waiting for transfers between devices, per_device(): lax.all_gather(grams[1].astype(jnp.bfloat16), 'own', axis=0, tiled=True)  105 us
    unnamed x48, waiting for transfers between devices  102 us
    reduce_scatter x1, waiting for transfers between devices, per_device(): lax.psum_scatter(partials[3], 'dp', scatter_dimension=0, tiled=True)  100 us
    reduce_scatter x1, waiting for transfers between devices, per_device(): lax.psum_scatter(partials[2], 'dp', scatter_dimension=1, tiled=True)  97.6 us
    all_gather x5, waiting for transfers between devices, per_device(): lax.all_gather(grams[3].astype(jnp.bfloat16), 'own', axis=0, tiled=True)  93.2 us
    all_gather x5, waiting for transfers between devices, per_device(): lax.all_gather(grams[4].astype(jnp.bfloat16), 'own', axis=0, tiled=True)  83.7 us
  transfers between devices with their start and end apart: 45, of which 41 were waited for; matrix products, arithmetic and copies ran while one was open for 9% of the time, Pallas kernels for 0%

commit v1 on v0

--- a/solution.py
+++ b/solution.py
@@ -259,7 +259,9 @@
             jnp.dot(iterate[index], columns[index].T, precision=highest) for index in range(5)
         ]
         grams = (
-            lax.psum(products[0].astype(jnp.bfloat16), "dp").astype(jnp.float32),
+            jnp.sum(
+                jax.lax.all_gather(products[0].astype(jnp.bfloat16), axis_name="dp"), axis=0
+            ).astype(jnp.float32),
             lax.psum(products[1].astype(jnp.bfloat16), "dp").astype(jnp.float32),
             lax.psum(products[2].astype(jnp.bfloat16), "dp").astype(jnp.float32),
             lax.psum(products[3].astype(jnp.bfloat16), "dp").astype(jnp.float32),

time: 2190 us -> 2260 us (1.032)
  waiting for transfers between devices: 1390 us -> 1440 us
    all_gather x5, waiting for transfers between devices: 65.5 us -> 133 us  [per_device(): lax.all_gather(grams[0].astype(jnp.bfloat16), 'own', axis=0, tiled=True)]
    all_gather x5, waiting for transfers between devices: 105 us -> 52 us  [per_device(): lax.all_gather(grams[1].astype(jnp.bfloat16), 'own', axis=0, tiled=True)]
    all_gather x0 -> x5, waiting for transfers between devices: none -> 49.5 us  [per_device(): jax.lax.all_gather(products[0].astype(jnp.bfloat16), axis_name='dp')]
    unnamed x48 -> x53, waiting for transfers between devices: 102 us -> 99.8 us
  transfers between devices with their start and end apart: 45 -> 50, of which waited for: 41 -> 46; matrix products, arithmetic and copies ran while one was open for 9% -> 11% of each run, Pallas kernels for 0% -> 0%
where the time goes in v1:
time: 2260 us; the launch traced here: 2250 us
  waiting for transfers between devices  1440 us (64%)
  blocking collectives  469 us (21%)
  matrix products  227 us (10%)
  local copies, waits for them, and re-layouts  46.1 us (2%)
  other arithmetic  40.5 us (2%)
  between operations  22.6 us (1%)
    psum x5, waiting for transfers between devices, per_device(): lax.psum(products[1].astype(jnp.bfloat16), 'dp').astype(jnp.float32)  298 us
    reduce_scatter x1, waiting for transfers between devices, per_device(): lax.psum_scatter(partials[4], 'dp', scatter_dimension=1, tiled=True)  145 us
    all_gather x5, waiting for transfers between devices, per_device(): lax.all_gather(grams[0].astype(jnp.bfloat16), 'own', axis=0, tiled=True)  133 us
    reduce_scatter x1, waiting for transfers between devices, per_device(): lax.psum_scatter(partials[3], 'dp', scatter_dimension=0, tiled=True)  100 us
    unnamed x53, waiting for transfers between devices  99.8 us
    reduce_scatter x1, waiting for transfers between devices, per_device(): lax.psum_scatter(partials[2], 'dp', scatter_dimension=1, tiled=True)  97.6 us
    all_gather x5, waiting for transfers between devices, per_device(): lax.all_gather(grams[3].astype(jnp.bfloat16), 'own', axis=0, tiled=True)  94.2 us
    all_gather x5, waiting for transfers between devices, per_device(): lax.all_gather(grams[4].astype(jnp.bfloat16), 'own', axis=0, tiled=True)  84.7 us
  transfers between devices with their start and end apart: 50, of which 46 were waited for; matrix products, arithmetic and copies ran while one was open for 11% of the time, Pallas kernels for 0%

profile of v1, /device:TPU:0, one launch (start us, length us, event | category | flops | bytes accessed | tf_op | source)
XLA Modules:
  0.0 2252.7 jit_solution(15174826304017888269)
XLA Ops:
  78.5 27.1 %all-reduce.1 = bf16[10752]{0:T(1024)(128)(2,1)S(1)} all-reduce(bf16[10752]{0:T(1024)(128)(2,1)S(1)} %dynamic-update-slice.1), channel_id=1, replica_groups=mesh['dp'=8,'own'=4] {'dp'}, use_global_device_ids=true, to_apply=%add.1 | all-reduce | flops 10752 | bytes 43008
  111.3 27.0 %all-gather.43.cloned.1.call-done = bf16[768,2304]{0,1:T(8,128)(2,1)} async-done(((bf16[768,288]{0,1:T(8,128)(2,1)}), bf16[768,2304]{0,1:T(8,128)(2,1)}) %all-gather.43.cloned.1.call-update) | async-done | bytes 3538960 | tf_op jit(solution)/shard_map/all_gather | solution.py:204
  167.1 47.7 %all-gather.47.cloned.1.call-done = bf16[768,3072]{1,0:T(8,128)(2,1)} async-done(((bf16[768,384]{1,0:T(8,128)(2,1)}), bf16[768,3072]{1,0:T(8,128)(2,1)}) %all-gather.47.cloned.1.call-update) | async-done | bytes 4718608 | tf_op jit(solution)/shard_map/all_gather | solution.py:206
  221.7 44.7 %all-gather.49.cloned.1.call-done = bf16[3072,768]{0,1:T(8,128)(2,1)} async-done(((bf16[384,768]{0,1:T(8,128)(2,1)}), bf16[3072,768]{0,1:T(8,128)(2,1)}) %all-gather.49.cloned.1.call-update) | async-done | bytes 4718608 | tf_op jit(solution)/shard_map/all_gather | solution.py:207
  376.7 39.8 %reduce-scatter.17.cloned.1.call-done = f32[768,288]{0,1:T(8,128)} async-done(((f32[768,2304]{0,1:T(8,128)}), f32[768,288]{0,1:T(8,128)}) %reduce-scatter.17.cloned.1.call-update) | async-done | bytes 884752 | tf_op jit(solution)/shard_map/reduce_scatter | solution.py:215
  419.2 97.6 %reduce-scatter.21.cloned.1.call-done = f32[768,384]{1,0:T(8,128)} async-done(((f32[768,3072]{1,0:T(8,128)}), f32[768,384]{1,0:T(8,128)}) %reduce-scatter.21.cloned.1.call-update) | async-done | bytes 1179664 | tf_op jit(solution)/shard_map/reduce_scatter | solution.py:217
  516.8 100.2 %reduce-scatter.25.cloned.1.call-done = f32[384,768]{0,1:T(8,128)} async-done(((f32[3072,768]{0,1:T(8,128)}), f32[384,768]{0,1:T(8,128)}) %reduce-scatter.25.cloned.1.call-update) | async-done | bytes 1179664 | tf_op jit(solution)/shard_map/reduce_scatter | solution.py:218
  617.1 144.6 %reduce-scatter.29.cloned.1.call-done = f32[768,576]{0,1:T(8,128)} async-done(((f32[768,4608]{0,1:T(8,128)}), f32[768,576]{0,1:T(8,128)}) %reduce-scatter.29.cloned.1.call-update) | async-done | bytes 1769488 | tf_op jit(solution)/shard_map/reduce_scatter | solution.py:219
  764.5 24.2 %reduce-scatter.33.cloned.1.call-done = f32[192,96]{1,0:T(8,128)} async-done(((f32[768,96]{1,0:T(8,128)}), f32[192,96]{1,0:T(8,128)}) %reduce-scatter.33.cloned.1.call-update) | async-done | bytes 73744
  790.3 30.6 %reduce-scatter.31.cloned.1.call-done = f32[192,288]{1,0:T(8,128)} async-done(((f32[768,288]{1,0:T(8,128)}), f32[192,288]{1,0:T(8,128)}) %reduce-scatter.31.cloned.1.call-update) | async-done | bytes 221200
  822.5 30.6 %reduce-scatter.23.cloned.1.call-done = f32[192,384]{1,0:T(8,128)} async-done(((f32[768,384]{1,0:T(8,128)}), f32[192,384]{1,0:T(8,128)}) %reduce-scatter.23.cloned.1.call-update) | async-done | bytes 294928 | tf_op jit(solution)/shard_map/reduce_scatter | solution.py:225
  854.8 30.5 %reduce-scatter.27.cloned.1.call-done = f32[384,192]{0,1:T(8,128)} async-done(((f32[384,768]{0,1:T(8,128)}), f32[384,192]{0,1:T(8,128)}) %reduce-scatter.27.cloned.1.call-update) | async-done | bytes 294928 | tf_op jit(solution)/shard_map/reduce_scatter | solution.py:226
  886.9 36.0 %reduce-scatter.35.cloned.1.call-done = f32[192,576]{1,0:T(8,128)} async-done(((f32[768,576]{1,0:T(8,128)}), f32[192,576]{1,0:T(8,128)}) %reduce-scatter.35.cloned.1.call-update) | async-done | bytes 442384
  924.7 39.7 %all-reduce.4 = (f32[]{:T(128)}, f32[]{:T(128)}, f32[]{:T(128)}, f32[]{:T(128)}, f32[]{:T(128)}) all-reduce(f32[]{:T(128)} %get-tuple-element.183, f32[]{:T(128)} %get-tuple-element.181, f32[]{:T(128)} %get-tuple-element.179, f32[]{:T(128)} %get-tuple-element.177, f32[]{:T(128)} %get-tuple-element.175), channel_id=1, replica_groups=mesh['dp'=8,'own'=4] {'dp','own'}, use_global_device_ids=true, to_apply=%region_36.37 | all-reduce | flops 5 | bytes 40 | tf_op jit(solution)/shard_map/psum | solution.py:236
  1016.8 59.6 %all-reduce.24.cloned.1.call-done = (bf16[192,768]{1,0:T(8,128)(2,1)}, bf16[192,768]{1,0:T(8,128)(2,1)}, bf16[192,768]{1,0:T(8,128)(2,1)}, bf16[192,768]{1,0:T(8,128)(2,1)}) async-done(((bf16[192,768]{1,0:T(8,128)(2,1)}, bf16[192,768]{1,0:T(8,128)(2,1)}, bf16[192,768]{1,0:T(8,128)(2,1)}, bf16[192,768]{1,0:T(8,128)(2,1)}), (bf16[192,768]{1,0:T(8,128)(2,1)}, bf16[192,768]{1,0:T(8,128)(2,1)}, ...) | async-done | bytes 1179664 | tf_op jit(solution)/shard_map/psum | solution.py:265
  1118.3 16.8 all-gather.81.cloned.1.call-done
  1232.7 59.7 %all-reduce.22.cloned.1.call-done = (bf16[192,768]{1,0:T(8,128)(2,1)}, bf16[192,768]{1,0:T(8,128)(2,1)}, bf16[192,768]{1,0:T(8,128)(2,1)}, bf16[192,768]{1,0:T(8,128)(2,1)}) async-done(((bf16[192,768]{1,0:T(8,128)(2,1)}, bf16[192,768]{1,0:T(8,128)(2,1)}, bf16[192,768]{1,0:T(8,128)(2,1)}, bf16[192,768]{1,0:T(8,128)(2,1)}), (bf16[192,768]{1,0:T(8,128)(2,1)}, bf16[192,768]{1,0:T(8,128)(2,1)}, ...) | async-done | bytes 1179664 | tf_op jit(solution)/shard_map/psum | solution.py:265
  1294.8 26.7 %all-gather.51.cloned.1.call-done = bf16[768,768]{1,0:T(8,128)(2,1)} async-done(((bf16[192,768]{1,0:T(8,128)(2,1)}), bf16[768,768]{1,0:T(8,128)(2,1)}) %all-gather.51.cloned.1.call-update) | async-done | bytes 1179664 | tf_op jit(solution)/shard_map/all_gather | solution.py:271
  1364.1 17.1 all-gather.83.cloned.1.call-done
  1395.9 15.5 all-gather.73.cloned.1.call-done
  1478.8 59.7 %all-reduce.20.cloned.1.call-done = (bf16[192,768]{1,0:T(8,128)(2,1)}, bf16[192,768]{1,0:T(8,128)(2,1)}, bf16[192,768]{1,0:T(8,128)(2,1)}, bf16[192,768]{1,0:T(8,128)(2,1)}) async-done(((bf16[192,768]{1,0:T(8,128)(2,1)}, bf16[192,768]{1,0:T(8,128)(2,1)}, bf16[192,768]{1,0:T(8,128)(2,1)}, bf16[192,768]{1,0:T(8,128)(2,1)}), (bf16[192,768]{1,0:T(8,128)(2,1)}, bf16[192,768]{1,0:T(8,128)(2,1)}, ...) | async-done | bytes 1179664 | tf_op jit(solution)/shard_map/psum | solution.py:265
  1540.7 26.8 %all-gather.53.cloned.1.call-done = bf16[768,768]{1,0:T(8,128)(2,1)} async-done(((bf16[192,768]{1,0:T(8,128)(2,1)}), bf16[768,768]{1,0:T(8,128)(2,1)}) %all-gather.53.cloned.1.call-update) | async-done | bytes 1179664 | tf_op jit(solution)/shard_map/all_gather | solution.py:271
  1610.2 17.1 all-gather.85.cloned.1.call-done
  1725.6 59.5 %all-reduce.18.cloned.1.call-done = (bf16[192,768]{1,0:T(8,128)(2,1)}, bf16[192,768]{1,0:T(8,128)(2,1)}, bf16[192,768]{1,0:T(8,128)(2,1)}, bf16[192,768]{1,0:T(8,128)(2,1)}) async-done(((bf16[192,768]{1,0:T(8,128)(2,1)}, bf16[192,768]{1,0:T(8,128)(2,1)}, bf16[192,768]{1,0:T(8,128)(2,1)}, bf16[192,768]{1,0:T(8,128)(2,1)}), (bf16[192,768]{1,0:T(8,128)(2,1)}, bf16[192,768]{1,0:T(8,128)(2,1)}, ...) | async-done | bytes 1179664 | tf_op jit(solution)/shard_map/psum | solution.py:265
  1787.3 26.8 %all-gather.55.cloned.1.call-done = bf16[768,768]{1,0:T(8,128)(2,1)} async-done(((bf16[192,768]{1,0:T(8,128)(2,1)}), bf16[768,768]{1,0:T(8,128)(2,1)}) %all-gather.55.cloned.1.call-update) | async-done | bytes 1179664 | tf_op jit(solution)/shard_map/all_gather | solution.py:271
  1857.5 16.4 all-gather.87.cloned.1.call-done
  1972.4 59.5 %all-reduce.16.cloned.1.call-done = (bf16[192,768]{1,0:T(8,128)(2,1)}, bf16[192,768]{1,0:T(8,128)(2,1)}, bf16[192,768]{1,0:T(8,128)(2,1)}, bf16[192,768]{1,0:T(8,128)(2,1)}) async-done(((bf16[192,768]{1,0:T(8,128)(2,1)}, bf16[192,768]{1,0:T(8,128)(2,1)}, bf16[192,768]{1,0:T(8,128)(2,1)}, bf16[192,768]{1,0:T(8,128)(2,1)}), (bf16[192,768]{1,0:T(8,128)(2,1)}, bf16[192,768]{1,0:T(8,128)(2,1)}, ...) | async-done | bytes 1179664 | tf_op jit(solution)/shard_map/psum | solution.py:265
  2032.0 29.0 %all-gather.57.cloned.1.call-done = bf16[768,768]{1,0:T(8,128)(2,1)} async-done(((bf16[192,768]{1,0:T(8,128)(2,1)}), bf16[768,768]{1,0:T(8,128)(2,1)}) %all-gather.57.cloned.1.call-update) | async-done | bytes 1179664 | tf_op jit(solution)/shard_map/all_gather | solution.py:271
  2094.5 29.4 %all-reduce.2 = f32[10752]{0:T(1024)} all-reduce(f32[10752]{0:T(1024)} %constant_dynamic-update-slice_fusion.10), channel_id=17, replica_groups=mesh['dp'=8,'own'=4] {'dp'}, use_global_device_ids=true, to_apply=%region_33.34.clone | all-reduce | flops 10752 | bytes 86016
  2157.4 26.2 %all-gather.99.cloned.1.call-done = bf16[768,768]{1,0:T(8,128)(2,1)} async-done(((bf16[192,768]{1,0:T(8,128)(2,1)}), bf16[768,768]{1,0:T(8,128)(2,1)}) %all-gather.99.cloned.1.call-update) | async-done | bytes 1179664 | tf_op jit(solution)/shard_map/all_gather | solution.py:283
  2186.0 26.8 %all-gather.89.cloned.1.call-done = bf16[768,768]{1,0:T(8,128)(2,1)} async-done(((bf16[192,768]{1,0:T(8,128)(2,1)}), bf16[768,768]{1,0:T(8,128)(2,1)}) %all-gather.89.cloned.1.call-update) | async-done | bytes 1179664 | tf_op jit(solution)/shard_map/all_gather | solution.py:280
  2219.0 23.9 %all-gather.59.cloned.1.call-done = bf16[768,768]{1,0:T(8,128)(2,1)} async-done(((bf16[192,768]{1,0:T(8,128)(2,1)}), bf16[768,768]{1,0:T(8,128)(2,1)}) %all-gather.59.cloned.1.call-update) | async-done | bytes 1179664 | tf_op jit(solution)/shard_map/all_gather | solution.py:271
  (607 shorter events, 913.3 us)
Async XLA Ops:
  36.4 125.9 %all-gather.45.cloned.1.call-start = ((), (), s32[]{:S(2)}) async-start(), calls=%async_computation.12 | async-start | bytes 1327104 | tf_op jit(solution)/shard_map/all_gather | solution.py:205
  44.6 170.2 %all-gather.47.cloned.1.call-start = ((), (), s32[]{:S(2)}) async-start(), calls=%async_computation.13 | async-start | bytes 5308416 | tf_op jit(solution)/shard_map/all_gather | solution.py:206
  56.4 210.0 %all-gather.49.cloned.1.call-start = ((), (), s32[]{:S(2)}) async-start(), calls=%async_computation.14 | async-start | bytes 5308416 | tf_op jit(solution)/shard_map/all_gather | solution.py:207
  67.1 307.7 %reduce-scatter.19.cloned.1.call-start = ((), (), s32[]{:S(2)}) async-start(), calls=%async_computation.16 | async-start | bytes 2654208 | tf_op jit(solution)/shard_map/reduce_scatter | solution.py:216
  294.5 122.1 %reduce-scatter.17.cloned.1.call-start = ((), (), s32[]{:S(2)}) async-start(), calls=%async_computation.15 | async-start | bytes 7962624 | tf_op jit(solution)/shard_map/reduce_scatter | solution.py:215
  340.5 176.3 %reduce-scatter.21.cloned.1.call-start = ((), (), s32[]{:S(2)}) async-start(), calls=%async_computation.17 | async-start | bytes 10616832 | tf_op jit(solution)/shard_map/reduce_scatter | solution.py:217
  348.6 268.4 %reduce-scatter.25.cloned.1.call-start = ((), (), s32[]{:S(2)}) async-start(), calls=%async_computation.19 | async-start | bytes 10616832 | tf_op jit(solution)/shard_map/reduce_scatter | solution.py:218
  359.1 402.5 %reduce-scatter.29.cloned.1.call-start = ((), (), s32[]{:S(2)}) async-start(), calls=%async_computation.21 | async-start | bytes 15925248 | tf_op jit(solution)/shard_map/reduce_scatter | solution.py:219
  374.7 414.1 %reduce-scatter.33.cloned.1.call-start = ((), (), s32[]{:S(2)}) async-start(), calls=%async_computation.53 | async-start | bytes 491520
  376.7 444.2 %reduce-scatter.31.cloned.1.call-start = ((), (), s32[]{:S(2)}) async-start(), calls=%async_computation.52 | async-start | bytes 1474560
  419.1 434.0 %reduce-scatter.23.cloned.1.call-start = ((), (), s32[]{:S(2)}) async-start(), calls=%async_computation.18 | async-start | bytes 1474560 | tf_op jit(solution)/shard_map/reduce_scatter | solution.py:225
  516.8 368.5 %reduce-scatter.27.cloned.1.call-start = ((), (), s32[]{:S(2)}) async-start(), calls=%async_computation.20 | async-start | bytes 1474560 | tf_op jit(solution)/shard_map/reduce_scatter | solution.py:226
  617.0 305.9 %reduce-scatter.35.cloned.1.call-start = ((), (), s32[]{:S(2)}) async-start(), calls=%async_computation.54 | async-start | bytes 2457600
  764.5 311.9 %all-reduce.24.cloned.1.call-start = ((), (), s32[]{:S(2)}) async-start(), calls=%async_computation.59 | async-start | bytes 2359296 | tf_op jit(solution)/shard_map/psum | solution.py:265
  1078.3 151.6 %all-gather.101.cloned.1.call-start = ((), (), s32[]{:S(2)}) async-start(), calls=%async_computation.47 | async-start | bytes 2654208 | tf_op jit(solution)/shard_map/all_gather | solution.py:263
  1093.6 198.9 %all-reduce.22.cloned.1.call-start = ((), (), s32[]{:S(2)}) async-start(), calls=%async_computation.58 | async-start | bytes 2359296 | tf_op jit(solution)/shard_map/psum | solution.py:265
  1232.7 119.1 %all-gather.63.cloned.1.call-start = ((), (), s32[]{:S(2)}) async-start(), calls=%async_computation.28 | async-start | bytes 1474560 | tf_op jit(solution)/shard_map/all_gather | solution.py:274
  1293.8 148.5 %all-gather.93.cloned.1.call-start = ((), (), s32[]{:S(2)}) async-start(), calls=%async_computation.43 | async-start | bytes 1474560 | tf_op jit(solution)/shard_map/all_gather | solution.py:283
  1294.4 181.6 %all-gather.103.cloned.1.call-start = ((), (), s32[]{:S(2)}) async-start(), calls=%async_computation.48 | async-start | bytes 2654208 | tf_op jit(solution)/shard_map/all_gather | solution.py:263
  1338.8 199.7 %all-reduce.20.cloned.1.call-start = ((), (), s32[]{:S(2)}) async-start(), calls=%async_computation.57 | async-start | bytes 2359296 | tf_op jit(solution)/shard_map/psum | solution.py:265
  1478.8 118.9 %all-gather.65.cloned.1.call-start = ((), (), s32[]{:S(2)}) async-start(), calls=%async_computation.29 | async-start | bytes 1474560 | tf_op jit(solution)/shard_map/all_gather | solution.py:274
  1539.3 118.8 %all-gather.75.cloned.1.call-start = ((), (), s32[]{:S(2)}) async-start(), calls=%async_computation.34 | async-start | bytes 1474560 | tf_op jit(solution)/shard_map/all_gather | solution.py:277
  1539.9 149.2 %all-gather.95.cloned.1.call-start = ((), (), s32[]{:S(2)}) async-start(), calls=%async_computation.44 | async-start | bytes 1474560 | tf_op jit(solution)/shard_map/all_gather | solution.py:283
  1540.6 182.1 %all-gather.105.cloned.1.call-start = ((), (), s32[]{:S(2)}) async-start(), calls=%async_computation.49 | async-start | bytes 2654208 | tf_op jit(solution)/shard_map/all_gather | solution.py:263
  1584.5 200.7 %all-reduce.18.cloned.1.call-start = ((), (), s32[]{:S(2)}) async-start(), calls=%async_computation.56 | async-start | bytes 2359296 | tf_op jit(solution)/shard_map/psum | solution.py:265
  1725.6 118.7 %all-gather.67.cloned.1.call-start = ((), (), s32[]{:S(2)}) async-start(), calls=%async_computation.30 | async-start | bytes 1474560 | tf_op jit(solution)/shard_map/all_gather | solution.py:274
  1785.7 119.2 %all-gather.77.cloned.1.call-start = ((), (), s32[]{:S(2)}) async-start(), calls=%async_computation.35 | async-start | bytes 1474560 | tf_op jit(solution)/shard_map/all_gather | solution.py:277
  1786.5 149.4 %all-gather.97.cloned.1.call-start = ((), (), s32[]{:S(2)}) async-start(), calls=%async_computation.45 | async-start | bytes 1474560 | tf_op jit(solution)/shard_map/all_gather | solution.py:283
  1787.2 182.3 %all-gather.107.cloned.1.call-start = ((), (), s32[]{:S(2)}) async-start(), calls=%async_computation.50 | async-start | bytes 2654208 | tf_op jit(solution)/shard_map/all_gather | solution.py:263
  1830.1 201.8 %all-reduce.16.cloned.1.call-start = ((), (), s32[]{:S(2)}) async-start(), calls=%async_computation.55 | async-start | bytes 2359296 | tf_op jit(solution)/shard_map/psum | solution.py:265
  1972.3 173.4 %all-gather.69.cloned.1.call-start = ((), (), s32[]{:S(2)}) async-start(), calls=%async_computation.31 | async-start | bytes 1474560 | tf_op jit(solution)/shard_map/all_gather | solution.py:274
  2079.2 133.7 %all-gather.89.cloned.1.call-start = ((), (), s32[]{:S(2)}) async-start(), calls=%async_computation.41 | async-start | bytes 1474560 | tf_op jit(solution)/shard_map/all_gather | solution.py:280
  (152 other events, 6345.6 us)
Sparse Core Ops, SparseCore 0:
  24.2 71.8 all-gather.40
  98.2 40.0 all-gather.42
  163.7 51.0 all-gather.46
  216.3 50.0 all-gather.48
  294.6 35.5 reduce-scatter.18
  340.6 75.8 reduce-scatter.16
  418.8 97.8 reduce-scatter.20
  519.1 97.8 reduce-scatter.24
  619.1 142.4 reduce-scatter.28
  792.1 28.7 reduce-scatter.30
  824.4 28.7 reduce-scatter.22
  856.5 28.7 reduce-scatter.26
  888.8 34.1 reduce-scatter.34
  1016.9 59.4 all-reduce.23
  1136.9 29.0 all-gather.70
  1167.7 28.4 all-gather.90
  1198.4 31.4 all-gather.100
  1233.1 59.3 all-reduce.21
  1323.2 28.5 all-gather.62
  1413.1 29.1 all-gather.92
  1444.5 31.4 all-gather.102
  1479.2 59.3 all-reduce.19
  1628.9 29.1 all-gather.74
  1659.9 29.0 all-gather.94
  1691.3 31.4 all-gather.104
  1725.8 59.3 all-reduce.17
  1875.8 29.1 all-gather.76
  1906.8 28.9 all-gather.96
  1938.1 31.4 all-gather.106
  1972.5 59.3 all-reduce.15
  2062.7 28.4 all-gather.68
  2093.2 32.3 all-gather.108
  (18 shorter events, 483.5 us)
